TPU v7x, 256 devices: a whole 4x4x8 slice. The times are simulated.
256 devices in a mesh: blk: 32 (over x, z_lo, core), uly: 8 (over y, z_hi).
Axes of the slice: x: 4, y: 4, z: 8 (z_hi: 2, z_lo: 4; z = z_hi * 4 + z_lo), core: 2. Of those that a mesh axis runs over, the one named last changes fastest.
Arguments:
- video_tokens: bfloat16 [12288, 3072], P(('blk', 'uly')), may hold values from -6 to 6
- text_tokens: bfloat16 [256, 3072], P('uly'), may hold values from -6 to 6
- video_modulation: bfloat16 [3, 3072], replicated, may hold values from -4 to 4
- text_modulation: bfloat16 [3, 3072], replicated, may hold values from -4 to 4
- video_projection: bfloat16 [3072, 3, 2048], P(None, None, 'uly'), may hold values from -0.109375 to 0.109375
- text_projection: bfloat16 [3072, 3, 2048], P(None, None, 'uly'), may hold values from -0.109375 to 0.109375
- video_output: bfloat16 [2048, 3072], P('uly'), may hold values from -0.125 to 0.125
- text_output: bfloat16 [2048, 3072], P('uly'), may hold values from -0.125 to 0.125
- video_gains: float32 [2, 128], replicated, may hold values from 1 to 12
- text_gains: float32 [2, 128], replicated, may hold values from 1 to 12
Outputs:
- video_attention: bfloat16 [12288, 3072], P(('blk', 'uly'))
- text_attention: bfloat16 [256, 3072], P('uly')
All inputs are finite; a program needn't handle non-finite values.
Results may differ from a plain program's by a relative error of at most 0.025.
The roundings to bfloat16 on the way count: a program that leaves them out, or rounds other values in their place, can miss the bound.
Values may be sent and summed in bfloat16 or wider, within the bound.
A program may use at most 128 MiB of HBM per device.

v0:
```python
import jax
import jax.numpy as jnp
from jax import lax
from jax.sharding import Mesh
from jax.sharding import PartitionSpec as P

HD = 128
BLK = ("blk_0", "blk_1", "blk_2")
ULY = ("uly_0", "uly_1")
BLK_ULY = ("blk_0", "blk_1", "blk_2", "uly_0", "uly_1")
EPS_NORM = 1e-06


def collected_together(x, axis):
    leaves = jax.tree.leaves(x)
    turns = sorted(range(len(leaves)), key=lambda k: -leaves[k].size)
    width = (1, *leaves[turns[0]].shape)[-1]
    lines = [
        jnp.pad(leaves[k].reshape(-1), (0, -leaves[k].size % width)).reshape(-1, width)
        for k in turns
    ]
    both, at, found = (lax.all_gather(jnp.concatenate(lines), axis), 0, {})
    for k, line in zip(turns, lines):
        slab = both[:, at : at + len(line)].reshape(len(both), -1)
        found[k] = slab[:, : leaves[k].size].reshape(-1, *leaves[k].shape)
        at += len(line)
    numbers = iter(range(len(leaves)))
    return jax.tree.map(lambda _: found[next(numbers)], x)


def merged_by_axis(x, axes, combine):
    for axis in axes:
        pieces = collected_together(
            jax.tree.map(
                lambda part, kind: part.astype(kind),
                x,
                jax.tree.map(lambda a: jnp.bfloat16 if a.dtype == jnp.float32 else a.dtype, x),
            ),
            axis,
        )
        widened = [
            jax.tree.map(lambda part, own: part[k].astype(own.dtype), pieces, x)
            for k in range(lax.axis_size(axis))
        ]
        x = widened[0]
        for partner_block in widened[1:]:
            x = combine(x, partner_block)
    return x


def summed_rows(terms, axes):
    subtotal = terms.astype(jnp.bfloat16)
    for axis in axes:
        subtotal = lax.psum_scatter(subtotal, axis, scatter_dimension=0, tiled=True)
    return subtotal.astype(jnp.float32)


def split_up(x, dim, length):
    before, after = (x.shape[:dim], x.shape[dim + 1 :])
    return jnp.moveaxis(x.reshape(*before, length, -1, *after), dim, 0)


def summed_on_arrival(x, axis, dim):
    length = lax.axis_size(axis)
    tiles = lax.all_to_all(split_up(x, dim, length), axis, 0, 0, tiled=True)
    return jnp.sum(tiles.astype(jnp.float32), axis=0)


def modulate(rows, factors):
    floats = rows.astype(jnp.float32)
    centre = floats - jnp.mean(floats, axis=-1, keepdims=True)
    spread = jnp.mean(centre * centre, axis=-1, keepdims=True)
    normed = centre / jnp.sqrt(spread + EPS_NORM)
    wide = factors.astype(jnp.float32)
    return (normed * (1.0 + wide[1]) + wide[0]).astype(jnp.bfloat16)


def head_norm(vectors, channel_gain):
    inverse = lax.rsqrt(jnp.mean(vectors * vectors, axis=-1, keepdims=True) + EPS_NORM)
    return (vectors * inverse * channel_gain).astype(jnp.bfloat16)


def project_rows(modded, weights, gains):
    mixture = jnp.einsum("td,dch->tch", modded, weights, preferred_element_type=jnp.float32)
    row_count, col_count = (mixture.shape[0], mixture.shape[2])
    per_head = mixture.reshape(row_count, 3, col_count // HD, HD)
    query_rows = head_norm(per_head[:, 0], gains[0]).reshape(row_count, col_count)
    key_rows = head_norm(per_head[:, 1], gains[1]).reshape(row_count, col_count)
    value_rows = per_head[:, 2].astype(jnp.bfloat16).reshape(row_count, col_count)
    return jnp.stack([query_rows, key_rows, value_rows], axis=1)


def block_scores(query_rows, key_rows):
    heads_here = query_rows.shape[1] // HD
    return jnp.einsum(
        "qhd,khd->hqk",
        query_rows.reshape(-1, heads_here, HD),
        key_rows.reshape(-1, heads_here, HD),
        preferred_element_type=jnp.float32,
    ) * HD ** (-0.5)


def weighted(weights, value_rows):
    heads_here = weights.shape[0]
    return jnp.einsum(
        "hqk,khd->hqd",
        weights.astype(jnp.bfloat16),
        value_rows.reshape(-1, heads_here, HD),
        preferred_element_type=jnp.float32,
    )


def opening(query_rows, key_rows, value_rows):
    scores = block_scores(query_rows, key_rows)
    highest = jnp.max(scores, axis=-1)
    weights = jnp.exp(scores - highest[..., None])
    return (highest, jnp.sum(weights, axis=-1), weighted(weights, value_rows))


def absorb(softmax_state, query_rows, key_rows, value_rows):
    highest, totals, weighted_sums = softmax_state
    scores = block_scores(query_rows, key_rows)
    raised = jnp.maximum(highest, jnp.max(scores, axis=-1))
    shrink = jnp.exp(highest - raised)
    weights = jnp.exp(scores - raised[..., None])
    return (
        raised,
        totals * shrink + jnp.sum(weights, axis=-1),
        weighted_sums * shrink[..., None] + weighted(weights, value_rows),
    )


def combine_states(earlier_state, later_state):
    raised = jnp.maximum(earlier_state[0], later_state[0])
    left_scale = jnp.exp(earlier_state[0] - raised)
    right_scale = jnp.exp(later_state[0] - raised)
    totals = earlier_state[1] * left_scale + later_state[1] * right_scale
    weighted_sums = (
        earlier_state[2] * left_scale[..., None] + later_state[2] * right_scale[..., None]
    )
    return (raised, totals, weighted_sums)


def finalize(softmax_state):
    result = softmax_state[2] / softmax_state[1][..., None]
    return jnp.transpose(result, (1, 0, 2)).reshape(result.shape[1], -1).astype(jnp.bfloat16)


def joint_attention(softmax_state, query_rows, pairs):
    shard_rows = pairs.shape[0]
    piece_rows = lax.all_gather(pairs, BLK, axis=0, tiled=True)
    turn_count = piece_rows.shape[0] // shard_rows
    turn_rows = piece_rows.shape[0] // turn_count

    def one_turn(turn_index, inner_state):
        sliced = lax.dynamic_slice_in_dim(piece_rows, turn_index * turn_rows, turn_rows, 0)
        return absorb(inner_state, query_rows, sliced[:, 0], sliced[:, 1])

    return lax.fori_loop(0, turn_count, one_turn, softmax_state)


def local(
    video_tokens,
    text_tokens,
    video_modulation,
    text_modulation,
    video_projection,
    text_projection,
    video_output,
    text_output,
    video_gains,
    text_gains,
):
    video_proj = project_rows(
        lax.all_gather(modulate(video_tokens, video_modulation), ULY, axis=0, tiled=True),
        video_projection,
        video_gains,
    )
    text_proj = project_rows(
        lax.all_gather(modulate(text_tokens, text_modulation), ULY, axis=0, tiled=True),
        text_projection,
        text_gains,
    )
    video_pairs = video_proj[:, 1:]
    video_state = opening(video_proj[:, 0], text_proj[:, 1], text_proj[:, 2])
    video_heads = finalize(joint_attention(video_state, video_proj[:, 0], video_pairs))
    text_state = opening(text_proj[:, 0], video_proj[:, 1], video_proj[:, 2])
    text_state = merged_by_axis(text_state, BLK, combine_states)
    text_heads = finalize(absorb(text_state, text_proj[:, 0], text_proj[:, 1], text_proj[:, 2]))
    video_summed = summed_rows(
        jnp.dot(video_heads, video_output, preferred_element_type=jnp.float32), ULY
    )
    text_summed = summed_on_arrival(
        jnp.dot(text_heads, text_output, preferred_element_type=jnp.float32).astype(jnp.bfloat16),
        ULY,
        0,
    )
    video_attention = (video_summed * video_modulation[2].astype(jnp.float32)).astype(jnp.bfloat16)
    text_attention = (text_summed * text_modulation[2].astype(jnp.float32)).astype(jnp.bfloat16)
    return (video_attention, text_attention)


def solution(mesh):
    torus = Mesh(mesh.devices.reshape(4, 4, 2, 4, 2), ("blk_0", "blk_1", "blk_2", "uly_0", "uly_1"))
    placed = (
        P(BLK_ULY, None),
        P(ULY, None),
        P(),
        P(),
        P(None, None, ULY),
        P(None, None, ULY),
        P(ULY, None),
        P(ULY, None),
        P(),
        P(),
    )
    return jax.shard_map(
        local,
        mesh=torus,
        in_specs=placed,
        out_specs=(P(BLK_ULY, None), P(ULY, None)),
        check_vma=False,
    )
```

profile of v0, /device:TPU:32, one launch (start us, length us, event | category | flops | bytes accessed | tf_op | source)
XLA Modules:
  0.0 410.6 jit_solution(2178064178969076653)
XLA Ops:
  8.9 1.1 convert_reduce_fusion.1
  10.0 1.2 fusion.17
  11.2 1.9 fusion.20
  14.6 80.3 %all-gather.7.cloned.1.call-done = bf16[384,3072]{1,0:T(8,128)(2,1)} async-done(((bf16[48,3072]{1,0:T(8,128)(2,1)}), bf16[384,3072]{1,0:T(8,128)(2,1)}) %all-gather.7.cloned.1.call-update) | async-done | bytes 2359312 | tf_op jit(solution)/shard_map/all_gather | solution.py:175
  94.9 5.3 %fusion.5 = f32[384,3,256]{0,2,1:T(8,128)S(1)} fusion(bf16[3072,3,256]{2,0,1:T(8,128)(2,1)} %param.16, bf16[384,3072]{1,0:T(8,128)(2,1)} %all-gather.7.cloned.1.call-done), kind=kOutput, calls=%fused_computation.14 | convolution fusion | flops 1811939328 | bytes 8257536 | tf_op jit(solution)/shard_map/td,dch->tch/dot_general | solution.py:84
  103.9 59.1 %all-gather.9.cloned.1.call-done = bf16[256,3072]{1,0:T(8,128)(2,1)} async-done(((bf16[32,3072]{1,0:T(8,128)(2,1)}), bf16[256,3072]{1,0:T(8,128)(2,1)}) %all-gather.9.cloned.1.call-update) | async-done | bytes 1572880 | tf_op jit(solution)/shard_map/all_gather | solution.py:180
  162.9 5.6 %fusion.7 = f32[256,3,256]{0,2,1:T(8,128)} fusion(bf16[3072,3,256]{2,0,1:T(8,128)(2,1)} %param.17, bf16[256,3072]{1,0:T(8,128)(2,1)} %all-gather.9.cloned.1.call-done), kind=kOutput, calls=%fused_computation.16 | convolution fusion | flops 1207959552 | bytes 7077888 | tf_op jit(solution)/shard_map/td,dch->tch/dot_general | solution.py:84
  171.9 1.2 fusion.156
  175.3 14.7 %all-gather = bf16[2080,128]{1,0:T(8,128)(2,1)S(1)} all-gather(bf16[520,128]{1,0:T(8,128)(2,1)S(1)} %pad_maximum_fusion.1), channel_id=2, replica_groups=mesh['blk_0'=4,'blk_1'=4,'blk_2'=2,'uly_0'=4,'uly_1'=2] {'blk_0'}, dimensions={0}, use_global_device_ids=true | all-gather | bytes 665600 | tf_op jit(solution)/shard_map/all_gather | solution.py:22
  191.7 52.5 %all-gather.11.cloned.1.call-done = bf16[12288,2,256]{0,2,1:T(8,128)(2,1)} async-done(((bf16[384,2,256]{0,2,1:T(8,128)(2,1)}), bf16[12288,2,256]{0,2,1:T(8,128)(2,1)}) %all-gather.11.cloned.1.call-update) | async-done | bytes 12582928 | tf_op jit(solution)/shard_map/all_gather | solution.py:151
  244.2 71.0 %while.17 = (s32[]{:T(128)}, f32[2,384]{1,0:T(2,128)S(1)}, f32[2,384]{1,0:T(2,128)S(1)}, f32[2,384,128]{2,1,0:T(8,128)S(1)}, bf16[12288,2,256]{0,2,1:T(8,128)(2,...) while((s32[]{:T(128)}, f32[2,384]{1,0:T(2,128)S(1)}, ...), condition=%wide.region_12.13_spmd, body=%wide.region_9.12_spmd.sunk | while | flops 152962560 | bytes 5750959 | solution.py:159
  246.4 1.1 constant_dynamic-slice_fusion.3
  248.7 1.1 constant_dynamic-slice_fusion.3
  250.9 1.1 constant_dynamic-slice_fusion.3
  253.1 1.1 constant_dynamic-slice_fusion.3
  255.3 1.1 constant_dynamic-slice_fusion.3
  257.5 1.1 constant_dynamic-slice_fusion.3
  259.8 1.1 constant_dynamic-slice_fusion.3
  262.0 1.1 constant_dynamic-slice_fusion.3
  264.2 1.1 constant_dynamic-slice_fusion.3
  266.4 1.1 constant_dynamic-slice_fusion.3
  268.6 1.1 constant_dynamic-slice_fusion.3
  270.9 1.1 constant_dynamic-slice_fusion.3
  273.1 1.1 constant_dynamic-slice_fusion.3
  275.3 1.1 constant_dynamic-slice_fusion.3
  277.5 1.1 constant_dynamic-slice_fusion.3
  279.7 1.1 constant_dynamic-slice_fusion.3
  282.0 1.1 constant_dynamic-slice_fusion.3
  284.2 1.1 constant_dynamic-slice_fusion.3
  286.4 1.1 constant_dynamic-slice_fusion.3
  288.6 1.1 constant_dynamic-slice_fusion.3
  290.8 1.1 constant_dynamic-slice_fusion.3
  293.1 1.1 constant_dynamic-slice_fusion.3
  295.3 1.1 constant_dynamic-slice_fusion.3
  297.5 1.1 constant_dynamic-slice_fusion.3
  299.7 1.1 constant_dynamic-slice_fusion.3
  301.9 1.1 constant_dynamic-slice_fusion.3
  304.2 1.1 constant_dynamic-slice_fusion.3
  306.4 1.1 constant_dynamic-slice_fusion.3
  308.6 1.1 constant_dynamic-slice_fusion.3
  315.5 2.2 convolution_convert_fusion
  317.7 15.7 %all-gather.1 = bf16[2080,128]{1,0:T(8,128)(2,1)S(1)} all-gather(bf16[520,128]{1,0:T(8,128)(2,1)S(1)} %pad_maximum_fusion.2), channel_id=3, replica_groups=mesh['blk_0'=4,'blk_1'=4,'blk_2'=2,'uly_0'=4,'uly_1'=2] {'blk_1'}, dimensions={0}, use_global_device_ids=true | all-gather | bytes 665600 | tf_op jit(solution)/shard_map/all_gather | solution.py:22
  334.0 2.0 all-gather.2
  337.8 1.8 convolution_convert_fusion.1
  339.5 6.8 %all-to-all-start = ((bf16[8,32,3072]{2,1,0:T(8,128)(2,1)}), bf16[8,32,3072]{2,1,0:T(8,128)(2,1)S(1)}, u32[]{:S(2)}, u32[]{:S(2)}) async-start(bf16[8,32,3072]{2,1,0:T(8,128)(2,1)} %bitcast.68), calls=%async_computation.2 | async-start | bytes 3145728 | tf_op jit(solution)/shard_map/all_to_all | solution.py:65
  346.4 4.9 %reduce-scatter.3.cloned.1.call-done = bf16[96,3072]{1,0:T(8,128)(2,1)} async-done(((bf16[384,3072]{1,0:T(8,128)(2,1)}), bf16[96,3072]{1,0:T(8,128)(2,1)}) %reduce-scatter.3.cloned.1.call-update) | async-done | bytes 589840 | tf_op jit(solution)/shard_map/reduce_scatter | solution.py:54
  351.4 50.1 %all-to-all-done = bf16[8,32,3072]{2,1,0:T(8,128)(2,1)S(1)} async-done(((bf16[8,32,3072]{2,1,0:T(8,128)(2,1)}), bf16[8,32,3072]{2,1,0:T(8,128)(2,1)S(1)}, u32[]{:S(2)}, u32[]{:S(2)}) %all-to-all-start) | async-done | bytes 1572896 | tf_op jit(solution)/shard_map/all_to_all | solution.py:65
  402.4 1.7 multiply_convert_fusion
  (303 shorter events, 55.6 us)
Async XLA Ops:
  7.2 308.3 %copy-start = (bf16[256,3072]{1,0:T(8,128)(2,1)S(1)}, bf16[256,3072]{1,0:T(8,128)(2,1)}, u32[]{:S(2)}) copy-start(bf16[256,3072]{1,0:T(8,128)(2,1)} %param.18) | copy-start | bytes 4718596
  7.2 6.0 %copy-start.9 = (bf16[3,3072]{1,0:T(4,128)(2,1)S(1)}, bf16[3,3072]{1,0:T(4,128)(2,1)}, u32[]{:S(2)}) copy-start(bf16[3,3072]{1,0:T(4,128)(2,1)} %param.15) | copy-start | bytes 55300
  7.2 6.0 %copy-start.3 = (bf16[32,3072]{1,0:T(8,128)(2,1)S(1)}, bf16[32,3072]{1,0:T(8,128)(2,1)}, u32[]{:S(2)}) copy-start(bf16[32,3072]{1,0:T(8,128)(2,1)} %param.13) | copy-start | bytes 589828
  7.2 7.4 %copy-start.10 = (f32[2,128]{1,0:T(2,128)S(1)}, f32[2,128]{1,0:T(2,128)}, u32[]{:S(2)}) copy-start(f32[2,128]{1,0:T(2,128)} %param.21) | copy-start | bytes 3076
  7.2 7.4 %copy-start.11 = (f32[2,128]{1,0:T(2,128)S(1)}, f32[2,128]{1,0:T(2,128)}, u32[]{:S(2)}) copy-start(f32[2,128]{1,0:T(2,128)} %param.20) | copy-start | bytes 3076
  7.2 87.7 %all-gather.7.cloned.1.call-start = ((), (), s32[]{:S(2)}) async-start(), calls=%async_computation.3 | async-start | bytes 2654208 | tf_op jit(solution)/shard_map/all_gather | solution.py:175
  13.1 149.8 %all-gather.9.cloned.1.call-start = ((), (), s32[]{:S(2)}) async-start(), calls=%async_computation.4 | async-start | bytes 1769472 | tf_op jit(solution)/shard_map/all_gather | solution.py:180
  14.5 229.7 %all-gather.11.cloned.1.call-start = ((), (), s32[]{:S(2)}) async-start(), calls=%async_computation.5 | async-start | bytes 12976128 | tf_op jit(solution)/shard_map/all_gather | solution.py:151
  102.1 0.9 copy-start.6
  103.8 247.5 %reduce-scatter.3.cloned.1.call-start = ((), (), s32[]{:S(2)}) async-start(), calls=%async_computation.6 | async-start | bytes 2949120 | tf_op jit(solution)/shard_map/reduce_scatter | solution.py:54
  171.3 1.8 copy-start.5
  174.9 15.6 %copy-start.1 = (f32[384,1,2,128]{3,0,2,1:T(8,128)S(1)}, f32[384,1,2,128]{3,0,2,1:T(8,128)}, u32[]{:S(2)}) copy-start(f32[384,1,2,128]{3,0,2,1:T(8,128)} %copy.54) | copy-start | bytes 1179652
  190.5 0.9 copy-start.7
  317.7 18.6 %copy-start.2 = (f32[2,256,256]{1,2,0:T(8,128)S(1)}, f32[2,256,256]{1,2,0:T(8,128)}, u32[]{:S(2)}) copy-start(f32[2,256,256]{1,2,0:T(8,128)} %get-tuple-element.171) | copy-start | bytes 1572868
  336.3 1.4 copy-start.4
  339.5 6.9 %copy-start.8 = (bf16[3,3072]{1,0:T(4,128)(2,1)S(1)}, bf16[3,3072]{1,0:T(4,128)(2,1)}, u32[]{:S(2)}) copy-start(bf16[3,3072]{1,0:T(4,128)(2,1)} %param.14) | copy-start | bytes 55300
  339.5 61.9 %all-to-all-start = ((bf16[8,32,3072]{2,1,0:T(8,128)(2,1)}), bf16[8,32,3072]{2,1,0:T(8,128)(2,1)S(1)}, u32[]{:S(2)}, u32[]{:S(2)}) async-start(bf16[8,32,3072]{2,1,0:T(8,128)(2,1)} %bitcast.68), calls=%async_computation.2 | async-start | bytes 3145728 | tf_op jit(solution)/shard_map/all_to_all | solution.py:65
  346.3 56.1 %reduce-scatter.5.cloned.1.call-start = ((), (), s32[]{:S(2)}) async-start(), calls=%async_computation.7 | async-start | bytes 884736 | tf_op jit(solution)/shard_map/reduce_scatter | solution.py:54
Sparse Core Ops, SparseCore 0:
  13.2 81.6 all-gather.6
  98.1 64.7 all-gather.8
  164.7 79.4 all-gather.10
  317.8 33.4 reduce-scatter.2
  353.7 44.8 reduce-scatter.4
where the time goes:
time: 412 us; the launch traced here: 411 us
  waiting for transfers between devices  247 us (60%)
  matrix products  46.4 us (11%)
  local copies, waits for them, and re-layouts  43.2 us (10%)
  blocking collectives  32.4 us (8%)
  other arithmetic  18.7 us (5%)
  between operations  14.3 us (3%)
  starting transfers between devices  7 us (2%)
    all_gather x1, waiting for transfers between devices, local(): lax.all_gather(modulate(video_tokens, video_modulation), ULY, axis=0, til...  80.3 us
    all_gather x1, waiting for transfers between devices, local(): lax.all_gather(modulate(text_tokens, text_modulation), ULY, axis=0, tiled...  59.1 us
    all_gather x1, waiting for transfers between devices, joint_attention(): piece_rows = lax.all_gather(pairs, BLK, axis=0, tiled=True)  52.5 us
    all_to_all x1, waiting for transfers between devices, summed_on_arrival(): tiles = lax.all_to_all(split_up(x, dim, length), axis, 0, 0, tiled=True)  50.1 us
    slice x32, local copies, waits for them, and re-layouts, one_turn(): return absorb(inner_state, query_rows, sliced[:, 0], sliced[:, 1])  34.2 us
    all_gather x3, blocking collectives, collected_together(): both, at, found = (lax.all_gather(jnp.concatenate(lines), axis), 0, {})  32.4 us
    dot_general x35, matrix products, weighted(): jnp.einsum('hqk,khd->hqd', weights.astype(jnp.bfloat16), value_rows.resha...  17.2 us
    dot_general x35, matrix products, block_scores(): jnp.einsum('qhd,khd->hqk', query_rows.reshape(-1, heads_here, HD), key_ro...  14.2 us
  transfers between devices with their start and end apart: 6, of which 5 were waited for; matrix products, arithmetic and copies ran while one was open for 7% of the time, Pallas kernels for 0%

commit v1 on v0

--- a/solution.py
+++ b/solution.py
@@ -177,7 +177,12 @@
         video_gains,
     )
     text_proj = project_rows(
-        lax.all_gather(modulate(text_tokens, text_modulation), ULY, axis=0, tiled=True),
+        jnp.concatenate(
+            lax.all_to_all(
+                jnp.stack([modulate(text_tokens, text_modulation)] * lax.axis_size(ULY)), ULY, 0, 0
+            ),
+            axis=0,
+        ),
         text_projection,
         text_gains,
     )

time: 412 us -> 383 us (0.930)
  waiting for transfers between devices: 247 us -> 206 us
  local copies, waits for them, and re-layouts: 43.2 us -> 49.6 us
  starting transfers between devices: 7 us -> 12.9 us
    all_gather x1 -> x0, waiting for transfers between devices: 59.1 us -> none  [local(): lax.all_gather(modulate(text_tokens, text_modulation), ULY, axis=0, tiled...]
    all_to_all x0 -> x1, waiting for transfers between devices: none -> 50 us  [local(): lax.all_to_all(jnp.stack([modulate(text_tokens, text_modulation)] * lax.a...]
    all_gather x1, waiting for transfers between devices: 52.5 us -> 20.1 us  [joint_attention(): piece_rows = lax.all_gather(pairs, BLK, axis=0, tiled=True)]
    dot_general x0 -> x1, local copies, waits for them, and re-layouts: none -> 6.83 us  [project_rows(): jnp.einsum('td,dch->tch', modded, weights, preferred_element_type=jnp.flo...]
    all_to_all x0 -> x1, starting transfers between devices: none -> 4.29 us  [local(): lax.all_to_all(jnp.stack([modulate(text_tokens, text_modulation)] * lax.a...]
where the time goes in v1:
time: 383 us; the launch traced here: 382 us
  waiting for transfers between devices  206 us (54%)
  local copies, waits for them, and re-layouts  49.6 us (13%)
  matrix products  47.2 us (12%)
  blocking collectives  30.9 us (8%)
  other arithmetic  19.3 us (5%)
  between operations  14.2 us (4%)
  starting transfers between devices  12.9 us (3%)
    all_gather x1, waiting for transfers between devices, local(): lax.all_gather(modulate(video_tokens, video_modulation), ULY, axis=0, til...  80.6 us
    all_to_all x1, waiting for transfers between devices, summed_on_arrival(): tiles = lax.all_to_all(split_up(x, dim, length), axis, 0, 0, tiled=True)  50.5 us
    all_to_all x1, waiting for transfers between devices, local(): lax.all_to_all(jnp.stack([modulate(text_tokens, text_modulation)] * lax.a...  50 us
    slice x32, local copies, waits for them, and re-layouts, one_turn(): return absorb(inner_state, query_rows, sliced[:, 0], sliced[:, 1])  34.2 us
    all_gather x3, blocking collectives, collected_together(): both, at, found = (lax.all_gather(jnp.concatenate(lines), axis), 0, {})  30.9 us
    all_gather x1, waiting for transfers between devices, joint_attention(): piece_rows = lax.all_gather(pairs, BLK, axis=0, tiled=True)  20.1 us
    dot_general x35, matrix products, weighted(): jnp.einsum('hqk,khd->hqd', weights.astype(jnp.bfloat16), value_rows.resha...  19.2 us
    dot_general x35, matrix products, block_scores(): jnp.einsum('qhd,khd->hqk', query_rows.reshape(-1, heads_here, HD), key_ro...  14.4 us
  transfers between devices with their start and end apart: 6, of which 5 were waited for; matrix products, arithmetic and copies ran while one was open for 7% of the time, Pallas kernels for 0%

profile of v1, /device:TPU:32, one launch (start us, length us, event | category | flops | bytes accessed | tf_op | source)
XLA Modules:
  0.0 381.6 jit_solution(18282657817665019766)
XLA Ops:
  8.8 1.1 convert_reduce_fusion.1
  10.0 1.2 fusion.15
  11.2 1.9 fusion.18
  14.3 80.6 %all-gather.6.cloned.1.call-done = bf16[384,3072]{1,0:T(8,128)(2,1)} async-done(((bf16[48,3072]{1,0:T(8,128)(2,1)}), bf16[384,3072]{1,0:T(8,128)(2,1)}) %all-gather.6.cloned.1.call-update) | async-done | bytes 2359312 | tf_op jit(solution)/shard_map/all_gather | solution.py:175
  94.9 5.3 %fusion.5 = f32[384,3,256]{0,2,1:T(8,128)S(1)} fusion(bf16[3072,3,256]{2,0,1:T(8,128)(2,1)} %param.16, bf16[384,3072]{1,0:T(8,128)(2,1)} %all-gather.6.cloned.1.call-done), kind=kOutput, calls=%fused_computation.14 | convolution fusion | flops 1811939328 | bytes 8257536 | tf_op jit(solution)/shard_map/td,dch->tch/dot_general | solution.py:84
  104.8 1.3 stack.4
  106.1 4.3 %all-to-all-start = ((bf16[8,32,3072]{2,1,0:T(8,128)(2,1)}), bf16[8,32,3072]{2,1,0:T(8,128)(2,1)}, u32[]{:S(2)}, u32[]{:S(2)}) async-start(bf16[8,32,3072]{2,1,0:T(8,128)(2,1)} %stack.4), calls=%async_computation | async-start | bytes 3145728 | tf_op jit(solution)/shard_map/all_to_all | solution.py:181
  110.5 6.8 %copy.60 = bf16[3,256,3072]{2,1,0:T(8,128)(2,1)} copy(bf16[3,256,3072]{1,2,0:T(8,128)(2,1)} %bitcast.619) | data formatting | bytes 9437184 | tf_op jit(solution)/shard_map/td,dch->tch/dot_general | solution.py:84
  117.3 50.0 %all-to-all-done = bf16[8,32,3072]{2,1,0:T(8,128)(2,1)} async-done(((bf16[8,32,3072]{2,1,0:T(8,128)(2,1)}), bf16[8,32,3072]{2,1,0:T(8,128)(2,1)}, u32[]{:S(2)}, u32[]{:S(2)}) %all-to-all-start) | async-done | bytes 1572896 | tf_op jit(solution)/shard_map/all_to_all | solution.py:181
  167.3 4.3 %fusion.144 = f32[256,3,2,128]{0,3,2,1:T(8,128)S(1)} fusion(bf16[256,3072,1,1]{1,0,3,2:T(8,128)(2,1)} %bitcast.13, bf16[3,2,128,3072]{3,2,1,0:T(8,128)(2,1)} %bitcast.620), kind=kOutput, calls=%fused_computation.247 | convolution fusion | flops 1207959552 | bytes 7077888 | tf_op jit(solution)/shard_map/td,dch->tch/dot_general | solution.py:84
  171.8 1.2 fusion.142
  174.4 1.2 copy.61
  175.6 1.3 convolution_convert_fusion.2
  177.6 14.2 %all-gather = bf16[2080,128]{1,0:T(8,128)(2,1)S(1)} all-gather(bf16[520,128]{1,0:T(8,128)(2,1)S(1)} %pad_maximum_fusion.1), channel_id=2, replica_groups=mesh['blk_0'=4,'blk_1'=4,'blk_2'=2,'uly_0'=4,'uly_1'=2] {'blk_0'}, dimensions={0}, use_global_device_ids=true | all-gather | bytes 665600 | tf_op jit(solution)/shard_map/all_gather | solution.py:22
  193.5 20.1 %all-gather.8.cloned.1.call-done = bf16[12288,2,256]{0,2,1:T(8,128)(2,1)} async-done(((bf16[384,2,256]{0,2,1:T(8,128)(2,1)}), bf16[12288,2,256]{0,2,1:T(8,128)(2,1)}) %all-gather.8.cloned.1.call-update) | async-done | bytes 12582928 | tf_op jit(solution)/shard_map/all_gather | solution.py:151
  213.6 71.0 %while.17 = (s32[]{:T(128)}, f32[2,384]{1,0:T(2,128)S(1)}, f32[2,384]{1,0:T(2,128)S(1)}, f32[2,384,128]{2,1,0:T(8,128)S(1)}, bf16[12288,2,256]{0,2,1:T(8,128)(2,...) while((s32[]{:T(128)}, f32[2,384]{1,0:T(2,128)S(1)}, ...), condition=%wide.region_12.13_spmd, body=%wide.region_9.12_spmd.sunk | while | flops 152962560 | bytes 5750959 | solution.py:159
  215.9 1.1 constant_dynamic-slice_fusion.3
  218.1 1.1 constant_dynamic-slice_fusion.3
  220.3 1.1 constant_dynamic-slice_fusion.3
  222.5 1.1 constant_dynamic-slice_fusion.3
  224.7 1.1 constant_dynamic-slice_fusion.3
  227.0 1.1 constant_dynamic-slice_fusion.3
  229.2 1.1 constant_dynamic-slice_fusion.3
  231.4 1.1 constant_dynamic-slice_fusion.3
  233.6 1.1 constant_dynamic-slice_fusion.3
  235.8 1.1 constant_dynamic-slice_fusion.3
  238.1 1.1 constant_dynamic-slice_fusion.3
  240.3 1.1 constant_dynamic-slice_fusion.3
  242.5 1.1 constant_dynamic-slice_fusion.3
  244.7 1.1 constant_dynamic-slice_fusion.3
  247.0 1.1 constant_dynamic-slice_fusion.3
  249.2 1.1 constant_dynamic-slice_fusion.3
  251.4 1.1 constant_dynamic-slice_fusion.3
  253.6 1.1 constant_dynamic-slice_fusion.3
  255.8 1.1 constant_dynamic-slice_fusion.3
  258.1 1.1 constant_dynamic-slice_fusion.3
  262.5 1.1 constant_dynamic-slice_fusion.3
  275.8 1.1 constant_dynamic-slice_fusion.3
  280.3 1.1 constant_dynamic-slice_fusion.3
  284.9 2.2 convolution_convert_fusion
  287.2 14.7 %all-gather.1 = bf16[2080,128]{1,0:T(8,128)(2,1)S(1)} all-gather(bf16[520,128]{1,0:T(8,128)(2,1)S(1)} %pad_maximum_fusion.2), channel_id=3, replica_groups=mesh['blk_0'=4,'blk_1'=4,'blk_2'=2,'uly_0'=4,'uly_1'=2] {'blk_1'}, dimensions={0}, use_global_device_ids=true | all-gather | bytes 665600 | tf_op jit(solution)/shard_map/all_gather | solution.py:22
  302.5 2.0 all-gather.2
  305.6 1.3 fusion.8
  307.0 1.8 convolution_convert_fusion.1
  308.8 8.5 %all-to-all-start.1 = ((bf16[8,32,3072]{2,1,0:T(8,128)(2,1)}), bf16[8,32,3072]{2,1,0:T(8,128)(2,1)S(1)}, u32[]{:S(2)}, u32[]{:S(2)}) async-start(bf16[8,32,3072]{2,1,0:T(8,128)(2,1)} %bitcast.71), calls=%async_computation.3 | async-start | bytes 3145728 | tf_op jit(solution)/shard_map/all_to_all | solution.py:65
  317.3 4.6 %reduce-scatter.3.cloned.1.call-done = bf16[96,3072]{1,0:T(8,128)(2,1)} async-done(((bf16[384,3072]{1,0:T(8,128)(2,1)}), bf16[96,3072]{1,0:T(8,128)(2,1)}) %reduce-scatter.3.cloned.1.call-update) | async-done | bytes 589840 | tf_op jit(solution)/shard_map/reduce_scatter | solution.py:54
  321.9 50.5 %all-to-all-done.1 = bf16[8,32,3072]{2,1,0:T(8,128)(2,1)S(1)} async-done(((bf16[8,32,3072]{2,1,0:T(8,128)(2,1)}), bf16[8,32,3072]{2,1,0:T(8,128)(2,1)S(1)}, u32[]{:S(2)}, u32[]{:S(2)}) %all-to-all-start.1) | async-done | bytes 1572896 | tf_op jit(solution)/shard_map/all_to_all | solution.py:65
  373.3 1.7 multiply_convert_fusion
  (304 shorter events, 59.1 us)
Async XLA Ops:
  7.2 277.8 %copy-start = (bf16[256,3072]{1,0:T(8,128)(2,1)S(1)}, bf16[256,3072]{1,0:T(8,128)(2,1)}, u32[]{:S(2)}) copy-start(bf16[256,3072]{1,0:T(8,128)(2,1)} %param.18) | copy-start | bytes 4718596
  7.2 6.0 %copy-start.14 = (f32[2,128]{1,0:T(2,128)S(1)}, f32[2,128]{1,0:T(2,128)}, u32[]{:S(2)}) copy-start(f32[2,128]{1,0:T(2,128)} %param.20) | copy-start | bytes 3076
  7.2 6.0 %copy-start.13 = (f32[2,128]{1,0:T(2,128)S(1)}, f32[2,128]{1,0:T(2,128)}, u32[]{:S(2)}) copy-start(f32[2,128]{1,0:T(2,128)} %param.21) | copy-start | bytes 3076
  7.2 87.7 %all-gather.6.cloned.1.call-start = ((), (), s32[]{:S(2)}) async-start(), calls=%async_computation.4 | async-start | bytes 2654208 | tf_op jit(solution)/shard_map/all_gather | solution.py:175
  13.1 200.5 %all-gather.8.cloned.1.call-start = ((), (), s32[]{:S(2)}) async-start(), calls=%async_computation.5 | async-start | bytes 12976128 | tf_op jit(solution)/shard_map/all_gather | solution.py:151
  13.8 0.6 copy-start.10
  101.6 15.8 %copy-start.3 = (bf16[384,1,2,128]{3,0,2,1:T(8,128)(2,1)}, bf16[384,1,2,128]{3,0,2,1:T(8,128)(2,1)S(1)}, u32[]{:S(2)}) copy-start(bf16[384,1,2,128]{3,0,2,1:T(8,128)(2,1)S(1)} %copy.63) | copy-start | bytes 589828
  101.6 2.6 copy-start.2
  106.1 61.2 %all-to-all-start = ((bf16[8,32,3072]{2,1,0:T(8,128)(2,1)}), bf16[8,32,3072]{2,1,0:T(8,128)(2,1)}, u32[]{:S(2)}, u32[]{:S(2)}) async-start(bf16[8,32,3072]{2,1,0:T(8,128)(2,1)} %stack.4), calls=%async_computation | async-start | bytes 3145728 | tf_op jit(solution)/shard_map/all_to_all | solution.py:181
  110.4 211.5 %reduce-scatter.3.cloned.1.call-start = ((), (), s32[]{:S(2)}) async-start(), calls=%async_computation.6 | async-start | bytes 2949120 | tf_op jit(solution)/shard_map/reduce_scatter | solution.py:54
  167.3 4.4 %copy-start.7 = (f32[128]{0:T(128)S(1)}, f32[128]{0:T(128)}, u32[]{:S(2)}) copy-start(f32[128]{0:T(128)} %get-tuple-element.165) | copy-start | bytes 1540
  167.3 4.4 %copy-start.9 = (f32[128]{0:T(128)S(1)}, f32[128]{0:T(128)}, u32[]{:S(2)}) copy-start(f32[128]{0:T(128)} %get-tuple-element.164) | copy-start | bytes 1540
  171.7 1.3 copy-start.11
  175.6 16.9 %copy-start.12 = (f32[128]{0:T(128)S(1)}, f32[128]{0:T(128)}, u32[]{:S(2)}) copy-start(f32[128]{0:T(128)} %get-tuple-element.176) | copy-start | bytes 1540
  176.8 15.8 %copy-start.8 = (f32[128]{0:T(128)S(1)}, f32[128]{0:T(128)}, u32[]{:S(2)}) copy-start(f32[128]{0:T(128)} %get-tuple-element.165) | copy-start | bytes 1540
  287.2 18.3 %copy-start.1 = (f32[2,256,256]{1,2,0:T(8,128)S(1)}, f32[2,256,256]{1,2,0:T(8,128)}, u32[]{:S(2)}) copy-start(f32[2,256,256]{1,2,0:T(8,128)} %get-tuple-element.171) | copy-start | bytes 1572868
  305.5 1.5 copy-start.4
  308.8 8.5 %copy-start.5 = (bf16[3,3072]{1,0:T(4,128)(2,1)S(1)}, bf16[3,3072]{1,0:T(4,128)(2,1)}, u32[]{:S(2)}) copy-start(bf16[3,3072]{1,0:T(4,128)(2,1)} %param.15) | copy-start | bytes 55300
  308.8 13.1 %copy-start.6 = (bf16[3,3072]{1,0:T(4,128)(2,1)S(1)}, bf16[3,3072]{1,0:T(4,128)(2,1)}, u32[]{:S(2)}) copy-start(bf16[3,3072]{1,0:T(4,128)(2,1)} %param.14) | copy-start | bytes 55300
  308.8 63.6 %all-to-all-start.1 = ((bf16[8,32,3072]{2,1,0:T(8,128)(2,1)}), bf16[8,32,3072]{2,1,0:T(8,128)(2,1)S(1)}, u32[]{:S(2)}, u32[]{:S(2)}) async-start(bf16[8,32,3072]{2,1,0:T(8,128)(2,1)} %bitcast.71), calls=%async_computation.3 | async-start | bytes 3145728 | tf_op jit(solution)/shard_map/all_to_all | solution.py:65
  317.2 56.1 %reduce-scatter.5.cloned.1.call-start = ((), (), s32[]{:S(2)}) async-start(), calls=%async_computation.7 | async-start | bytes 884736 | tf_op jit(solution)/shard_map/reduce_scatter | solution.py:54
Sparse Core Ops, SparseCore 0:
  13.2 81.6 all-gather.5
  102.8 110.7 all-gather.7
  287.3 34.5 reduce-scatter.2
  324.2 45.1 reduce-scatter.4
